TPU v7x, 32 devices: a whole 2x2x4 slice. The times are simulated.
32 devices in a mesh: dp: 8 (over z, y), tensor: 4 (over x, core).
Axes of the slice: x: 2, y: 2, z: 4, core: 2. Of those that a mesh axis runs over, the one named last changes fastest.
Arguments:
- token_ids: int32 [256, 512], P('dp'), may hold values from 0 to 31999
- lengths: int32 [256], P('dp'), may hold values from 128 to 512
- table: bfloat16 [1024, 32000], P('tensor'), may hold values from -6 to 6
- cotangent: bfloat16 [256, 1024, 256], P('dp', 'tensor'), may hold values from -6 to 6
- proj_a: bfloat16 [1024, 64], P('tensor'), may hold values from -0.1875 to 0.1875
- proj_b: bfloat16 [1024, 5, 64], P('tensor'), may hold values from -0.078125 to 0.078125
Outputs:
- similarity: float32 [256, 256], P(('dp', 'tensor'))
Inputs may be any that keep to these rules, and one draw needn't show every extreme that they name: `lengths`: each recipe has at least a quarter of its positions live.
All inputs are finite; a program needn't handle non-finite values.
Results may differ from a plain program's by a relative error of at most 0.0012.
Values may be sent and summed in bfloat16 or wider, within the bound.
A program may use at most 320 MiB of HBM per device.

v0:
```python
import jax
import jax.numpy as jnp
from jax import lax
from jax.sharding import PartitionSpec as P


def project_table(table, proj_b):
    chans, taps, width = proj_b.shape
    flat = proj_b.reshape(chans, taps * width)
    return lax.dot_general(
        table, flat, (((0,), (0,)), ((), ())), preferred_element_type=jnp.float32
    )


def right_block(ids_b, len_b, projected, taps, width):
    count, seqlen = ids_b.shape
    steps_out = seqlen // 2
    rows = jnp.take(projected, ids_b.reshape(count * seqlen), axis=0)
    pos = jnp.arange(seqlen, dtype=jnp.int32)
    keep = (pos[None, :] < len_b[:, None]).astype(jnp.float32).reshape(count * seqlen, 1)
    rows = (rows * keep).reshape(count, steps_out, 2, taps, width)
    even = rows[:, :, 0]
    odd = rows[:, :, 1]
    centre = even[:, :, 2] + odd[:, :, 3]
    before = even[:, :, 0] + odd[:, :, 1]
    after = even[:, :, 4]
    zero_row = jnp.zeros((count, 1, width), jnp.float32)
    before = jnp.concatenate([zero_row, before[:, :-1]], axis=1)
    after = jnp.concatenate([after[:, 1:], zero_row], axis=1)
    return centre + before + after


def left_block(len_b, delta_b, proj_a):
    steps_out = delta_b.shape[2]
    outpos = 2 * jnp.arange(steps_out, dtype=jnp.int32)
    tkeep = (outpos[None, :] < len_b[:, None]).astype(delta_b.dtype)
    masked = delta_b * tkeep[:, None, :]
    return jnp.einsum("nct,ca->nat", masked, proj_a, preferred_element_type=jnp.float32)


def local(token_ids, lengths, table, cotangent, proj_a, proj_b):
    recipes_here, seqlen = token_ids.shape
    width = proj_a.shape[1]
    taps = proj_b.shape[1]
    steps_out = seqlen // 2
    tensor_count = lax.axis_size("tensor")
    block_rows = 16
    nblk = recipes_here // block_rows
    ids_r = token_ids.reshape(nblk, block_rows, seqlen)
    len_r = lengths.reshape(nblk, block_rows)
    total_feats = width * width
    projected = project_table(table, proj_b)

    def right_one(parts):
        return right_block(parts[0], parts[1], projected, taps, width)

    right_part = lax.map(right_one, (ids_r, len_r)).reshape(recipes_here, steps_out, width)
    del_r = cotangent.reshape(nblk, block_rows, cotangent.shape[1], steps_out)

    def left_one(parts):
        return left_block(parts[0], parts[1], proj_a)

    left_part = lax.map(left_one, (len_r, del_r)).reshape(recipes_here, width, steps_out)
    left_rows = lax.psum_scatter(left_part, "tensor", scatter_dimension=1, tiled=True)
    right_own = lax.psum_scatter(right_part, "tensor", scatter_dimension=0, tiled=True)
    right_full = lax.all_gather(right_own, "tensor", axis=0, tiled=True)
    raw = jnp.einsum("nat,ntb->nab", left_rows, right_full, precision=lax.Precision.HIGHEST)
    squares = lax.psum(jnp.sum(raw * raw, axis=(1, 2)), "tensor")
    scale = lax.rsqrt(squares / total_feats + 1e-06)
    panel = (raw * scale[:, None, None]).astype(jnp.bfloat16)
    panel_flat = panel.reshape(recipes_here, width // tensor_count * width)
    terms = lax.dot_general(
        panel_flat,
        lax.all_gather(panel_flat, "dp", axis=0, tiled=True),
        (((1,), (1,)), ((), ())),
        preferred_element_type=jnp.float32,
    )
    summed = lax.psum_scatter(terms, "tensor", scatter_dimension=0, tiled=True)
    return summed * (1.0 / total_feats)


def solution(mesh):
    placed = (
        P("dp", None),
        P("dp"),
        P("tensor", None),
        P("dp", "tensor", None),
        P("tensor", None),
        P("tensor", None, None),
    )
    return jax.shard_map(
        local, mesh=mesh, in_specs=placed, out_specs=P(("dp", "tensor"), None), check_vma=False
    )
```

profile of v0, /device:TPU:0, one launch (start us, length us, event | category | flops | bytes accessed | tf_op | source)
XLA Modules:
  0.0 506.3 jit_solution(3134965903721458761)
XLA Ops:
  6.5 0.0 copy-start
  6.5 0.0 reduce-scatter.6.cloned.1.call-start
  6.5 0.8 reshape.131
  7.3 0.2 copy-done
  7.5 27.1 %fusion.16 = f32[32000,320]{1,0:T(8,128)} fusion(bf16[256,32000]{1,0:T(8,128)(2,1)} %param.12, bf16[256,320]{0,1:T(8,128)(2,1)S(1)} %bitcast.90), kind=kOutput, calls=%fused_computation.39 | convolution fusion | flops 5242880000 | bytes 57507840 | tf_op jit(solution)/shard_map/dot_general | solution.py:10
  34.6 308.5 %while.21 = (s32[]{:T(128)}, f32[2,16,256,64]{2,3,1,0:T(8,128)}, s32[2,16,512]{2,1,0:T(8,128)S(1)}, f32[32000,320]{1,0:T(8,128)}, s32[2,16]{1,0:T(2,128)S(1)}, /*index=5*/s32[]{:T(128)}) while((s32[]{:T(128)}, f32[2,16,256,64]{2,3,1,0:T(8,128)}, s32[2,16,512]{2,1,0:T(8,128)S(1)}, f32[32000,320]{1,0:T(8,128)}, s32[2,16]{1,0:T(2,128)S(1)}, ...), condition=%wide.region_4.5_spmd, body=%wide.region_3.4_spmd.sunk | while | flops 6406146 | bytes 115950352 | solution.py:57
  34.7 48.5 %gather_fusion = f32[8192,320]{1,0:T(8,128)} fusion(f32[32000,320]{1,0:T(8,128)} %get-tuple-element.221, s32[8192]{0:T(1024)S(1)} %broadcast_clamp_fusion.2), kind=kCustom, calls=%fused_computation.clone.1 | custom fusion | bytes 21004288 | tf_op jit(solution)/shard_map/while/body/eval_jaxpr/jit(_take)/gather | solution.py:18
  83.2 21.7 %gather.11 = f32[16,256,2,5,64]{4,3,2,1,0:T(8,128)} reshape(f32[8192,320]{1,0:T(8,128)} %gather_fusion) | data formatting | bytes 20971520 | tf_op jit(solution)/shard_map/while/body/eval_jaxpr/jit(_take)/gather | solution.py:18
  104.9 0.1 copy.55
  105.1 0.3 compare_and_fusion.2
  105.4 2.0 copy.56
  107.5 0.1 fusion.39
  107.5 0.6 copy.54
  108.2 25.0 %select_multiply_fusion.2 = f32[16,256,2,5,64]{4,3,2,1,0:T(8,128)} fusion(f32[16,256,2,5,64]{4,3,2,1,0:T(8,128)} %gather.11, f32[16,256,2]{2,1,0:T(8,128)S(1)} %copy.54, pred[16,256,2]{2,1,0:T(8,128)(4,1)S(1)} %copy.56), kind=kLoop, calls=%fused_computation.13.clone.1 | loop fusion | flops 5242880 | bytes 21012480 | tf_op jit(solution)/shard_map/while/body/eval_jaxpr/mul | solution.py:21
  133.2 22.0 %fusion.40 = (f32[16,256,1,5,64]{4,3,2,1,0:T(8,128)}, f32[16,256,5,64]{3,2,1,0:T(8,128)}) fusion(f32[16,256,2,5,64]{4,3,2,1,0:T(8,128)} %select_multiply_fusion.2), kind=kLoop, calls=%fused_computation.37.clone.1 | loop fusion | bytes 20971520 | tf_op jit(solution)/shard_map/while/body/eval_jaxpr/slice | solution.py:22
  155.1 11.7 %copy.57 = f32[16,256,1,5,64]{4,1,0,3,2:T(8,128)} copy(f32[16,256,1,5,64]{4,3,2,1,0:T(8,128)} %get-tuple-element.182) | data formatting | bytes 10485760 | tf_op jit(solution)/shard_map/while
  166.8 2.5 fusion.41
  169.3 15.2 %slice_add_fusion.3 = (f32[16,256,1,64]{3,2,1,0:T(1,128)S(1)}, f32[16,256,1,64]{3,2,1,0:T(1,128)S(1)}) fusion(f32[16,256,1,64]{3,2,1,0:T(1,128)S(1)} %bitcast.95, f32[16,256,5,64]{3,2,1,0:T(8,128)} %get-tuple-element.184), kind=kLoop, calls=%fused_computation.17.clone.1 | loop fusion | flops 262144 | bytes 5242880 | tf_op jit(solution)/shard_map/while/body/eval_jaxpr/add | solution.py:25
  184.6 0.2 slice.66
  184.8 2.4 fusion.42
  187.2 0.6 copy.58
  187.8 1.1 constant_dynamic-update-slice_fusion.2
  188.9 48.5 %gather_fusion = f32[8192,320]{1,0:T(8,128)} fusion(f32[32000,320]{1,0:T(8,128)} %get-tuple-element.221, s32[8192]{0:T(1024)S(1)} %broadcast_clamp_fusion.2), kind=kCustom, calls=%fused_computation.clone.1 | custom fusion | bytes 21004288 | tf_op jit(solution)/shard_map/while/body/eval_jaxpr/jit(_take)/gather | solution.py:18
  237.5 21.7 %gather.11 = f32[16,256,2,5,64]{4,3,2,1,0:T(8,128)} reshape(f32[8192,320]{1,0:T(8,128)} %gather_fusion) | data formatting | bytes 20971520 | tf_op jit(solution)/shard_map/while/body/eval_jaxpr/jit(_take)/gather | solution.py:18
  259.2 0.1 copy.55
  259.3 0.3 compare_and_fusion.2
  259.6 2.0 copy.56
  261.7 0.1 fusion.39
  261.8 0.6 copy.54
  262.4 25.0 %select_multiply_fusion.2 = f32[16,256,2,5,64]{4,3,2,1,0:T(8,128)} fusion(f32[16,256,2,5,64]{4,3,2,1,0:T(8,128)} %gather.11, f32[16,256,2]{2,1,0:T(8,128)S(1)} %copy.54, pred[16,256,2]{2,1,0:T(8,128)(4,1)S(1)} %copy.56), kind=kLoop, calls=%fused_computation.13.clone.1 | loop fusion | flops 5242880 | bytes 21012480 | tf_op jit(solution)/shard_map/while/body/eval_jaxpr/mul | solution.py:21
  287.4 22.0 %fusion.40 = (f32[16,256,1,5,64]{4,3,2,1,0:T(8,128)}, f32[16,256,5,64]{3,2,1,0:T(8,128)}) fusion(f32[16,256,2,5,64]{4,3,2,1,0:T(8,128)} %select_multiply_fusion.2), kind=kLoop, calls=%fused_computation.37.clone.1 | loop fusion | bytes 20971520 | tf_op jit(solution)/shard_map/while/body/eval_jaxpr/slice | solution.py:22
  309.4 11.7 %copy.57 = f32[16,256,1,5,64]{4,1,0,3,2:T(8,128)} copy(f32[16,256,1,5,64]{4,3,2,1,0:T(8,128)} %get-tuple-element.182) | data formatting | bytes 10485760 | tf_op jit(solution)/shard_map/while
  321.1 2.5 fusion.41
  323.6 15.2 %slice_add_fusion.3 = (f32[16,256,1,64]{3,2,1,0:T(1,128)S(1)}, f32[16,256,1,64]{3,2,1,0:T(1,128)S(1)}) fusion(f32[16,256,1,64]{3,2,1,0:T(1,128)S(1)} %bitcast.95, f32[16,256,5,64]{3,2,1,0:T(8,128)} %get-tuple-element.184), kind=kLoop, calls=%fused_computation.17.clone.1 | loop fusion | flops 262144 | bytes 5242880 | tf_op jit(solution)/shard_map/while/body/eval_jaxpr/add | solution.py:25
  338.8 0.2 slice.66
  339.0 2.4 fusion.42
  341.4 0.6 copy.58
  342.0 1.1 constant_dynamic-update-slice_fusion.2
  343.1 0.0 reduce-scatter.6.cloned.1.call-update
  343.1 0.0 reduce-scatter.4.cloned.1.call-start
  343.2 0.7 copy-done.4
  343.8 4.5 while.20
  343.9 0.1 compare_convert_fusion.2
  343.9 2.1 fusion.36
  346.1 0.1 compare_convert_fusion.2
  346.2 2.2 fusion.36
  348.3 1.3 copy-done.2
  349.6 0.0 reduce-scatter.4.cloned.1.call-update
  349.7 0.0 all-gather.2.cloned.1.call-start
  349.7 27.7 %reduce-scatter.6.cloned.1.call-done = f32[8,256,64]{1,2,0:T(8,128)} async-done(((f32[32,256,64]{1,2,0:T(8,128)}), f32[8,256,64]{1,2,0:T(8,128)}) %reduce-scatter.6.cloned.1.call-update) | async-done | bytes 524304 | tf_op jit(solution)/shard_map/reduce_scatter | solution.py:65
  377.4 0.0 all-gather.2.cloned.1.call-update
  377.4 0.0 copy-start.1
  377.4 0.0 reduce-scatter.8.cloned.1.call-start
  377.5 34.1 %reduce-scatter.4.cloned.1.call-done = f32[32,16,256]{2,1,0:T(8,128)} async-done(((f32[32,64,256]{2,1,0:T(8,128)}), f32[32,16,256]{2,1,0:T(8,128)}) %reduce-scatter.4.cloned.1.call-update) | async-done | bytes 524304 | tf_op jit(solution)/shard_map/reduce_scatter | solution.py:64
  411.6 24.2 %all-gather.2.cloned.1.call-done = f32[32,256,64]{1,2,0:T(8,128)} async-done(((f32[8,256,64]{1,2,0:T(8,128)}), f32[32,256,64]{1,2,0:T(8,128)}) %all-gather.2.cloned.1.call-update) | async-done | bytes 2097168 | tf_op jit(solution)/shard_map/all_gather | solution.py:66
  435.8 3.7 multiply_reduce_fusion
  439.4 5.9 %psum.7 = f32[32]{0:T(128)S(1)} all-reduce(f32[32]{0:T(128)S(1)} %get-tuple-element.112), channel_id=1, replica_groups=mesh['dp'=8,'tensor'=4] {'tensor'}, use_global_device_ids=true, to_apply=%region_7.8 | all-reduce | flops 32 | bytes 256 | tf_op jit(solution)/shard_map/psum | solution.py:68
  445.3 0.1 multiply_convert_fusion
  445.4 0.1 reshape.136
  445.6 31.8 %all_gather.7 = bf16[256,1024]{1,0:T(8,128)(2,1)S(1)} all-gather(bf16[32,1024]{1,0:T(8,128)(2,1)S(1)} %reshape.136), channel_id=1, replica_groups=mesh['dp'=8,'tensor'=4] {'dp'}, dimensions={0}, use_global_device_ids=true | all-gather | bytes 589824 | tf_op jit(solution)/shard_map/all_gather | solution.py:74
  477.4 0.9 fusion.17
  478.3 0.0 reduce-scatter.8.cloned.1.call-update
  478.3 20.2 %reduce-scatter.8.cloned.1.call-done = f32[8,256]{1,0:T(8,128)} async-done(((f32[32,256]{1,0:T(8,128)}), f32[8,256]{1,0:T(8,128)}) %reduce-scatter.8.cloned.1.call-update) | async-done | bytes 8208 | tf_op jit(solution)/shard_map/reduce_scatter | solution.py:78
  498.5 1.3 broadcast_multiply_fusion
  (24 shorter events, 0.2 us)
Async XLA Ops:
  6.5 0.9 copy-start
  6.5 370.9 %reduce-scatter.6.cloned.1.call-start = ((), (), s32[]{:S(2)}) async-start(), calls=%async_computation.4 | async-start | bytes 2621440 | tf_op jit(solution)/shard_map/reduce_scatter | solution.py:65
  7.5 27.1 %copy-start.3 = (s32[32,512]{1,0:T(8,128)S(1)}, s32[32,512]{1,0:T(8,128)}, u32[]{:S(2)}) copy-start(s32[32,512]{1,0:T(8,128)} %param.10) | copy-start | bytes 196612
  343.1 0.8 copy-start.4
  343.1 68.4 %reduce-scatter.4.cloned.1.call-start = ((), (), s32[]{:S(2)}) async-start(), calls=%async_computation.3 | async-start | bytes 2621440 | tf_op jit(solution)/shard_map/reduce_scatter | solution.py:64
  348.3 1.3 copy-start.2
  349.7 86.1 %all-gather.2.cloned.1.call-start = ((), (), s32[]{:S(2)}) async-start(), calls=%async_computation.5 | async-start | bytes 2621440 | tf_op jit(solution)/shard_map/all_gather | solution.py:66
  377.4 122.4 %copy-start.1 = (bf16[256,5,64]{0,2,1:T(8,128)(2,1)S(1)}, bf16[256,5,64]{0,2,1:T(8,128)(2,1)}, u32[]{:S(2)}) copy-start(bf16[256,5,64]{0,2,1:T(8,128)(2,1)} %param.15) | copy-start | bytes 491524
  377.4 121.1 %reduce-scatter.8.cloned.1.call-start = ((), (), s32[]{:S(2)}) async-start(), calls=%async_computation.6 | async-start | bytes 40960 | tf_op jit(solution)/shard_map/reduce_scatter | solution.py:78
Sparse Core Ops, SparseCore 0:
  343.2 34.1 reduce-scatter.5
  380.1 31.4 reduce-scatter.3
  413.1 22.5 all-gather.1
  478.4 20.0 reduce-scatter.7
where the time goes:
time: 508 us; the launch traced here: 506 us
  local copies, waits for them, and re-layouts  225 us (44%)
  waiting for transfers between devices  106 us (21%)
  other arithmetic  87.7 us (17%)
  blocking collectives  37.7 us (7%)
  matrix products  35.9 us (7%)
  between operations  13.2 us (3%)
    gather x4, local copies, waits for them, and re-layouts, right_block(): rows = jnp.take(projected, ids_b.reshape(count * seqlen), axis=0)  141 us
    mul x2, other arithmetic, right_block(): rows = (rows * keep).reshape(count, steps_out, 2, taps, width)  50 us
    slice x2, local copies, waits for them, and re-layouts, right_block(): even = rows[:, :, 0]  44 us
    reduce_scatter x1, waiting for transfers between devices, local(): lax.psum_scatter(left_part, 'tensor', scatter_dimension=1, tiled=True)  34.1 us
    all_gather x1, blocking collectives, local(): lax.all_gather(panel_flat, 'dp', axis=0, tiled=True)  31.8 us
    add x2, other arithmetic, right_block(): before = even[:, :, 0] + odd[:, :, 1]  30.5 us
    reduce_scatter x1, waiting for transfers between devices, local(): lax.psum_scatter(right_part, 'tensor', scatter_dimension=0, tiled=True)  27.7 us
    dot_general x1, matrix products, project_table(): lax.dot_general(table, flat, (((0,), (0,)), ((), ())), preferred_element_...  27.1 us
  transfers between devices with their start and end apart: 4, of which 4 were waited for; matrix products, arithmetic and copies ran while one was open for 1% of the time, Pallas kernels for 0%

commit v1 on v0

v1 whole, which is shorter than its diff:
```python
import functools

import jax
import jax.numpy as jnp
from jax import lax
from jax.experimental import pallas as pl
from jax.experimental.pallas import tpu as pltpu
from jax.sharding import PartitionSpec as P

LANES = 128
UNROLL = 8
PAD = 8


def right_kernel(vocab, vblocks, group, steps_out, ids_ref, live_ref, table_ref, w_ref, out_ref, rows, near, far):
    step = pl.program_id(0)
    vblk = table_ref.shape[1]

    @pl.when(step < vblocks)
    def _():
        base = pl.multiple_of(step * vblk, LANES)
        part = lax.dot_general(
            table_ref[...], w_ref[...], (((0,), (0,)), ((), ())), preferred_element_type=jnp.float32
        )
        for col in range(3):
            rows[col, pl.ds(base, vblk), :] = part[:, col * LANES:(col + 1) * LANES]

    @pl.when(step == vblocks)
    def _():
        for col in range(3):
            rows[col, pl.ds(vocab, PAD), :] = jnp.zeros((PAD, LANES), jnp.float32)
        for side in range(2):
            near[side, pl.ds(0, PAD), :] = jnp.zeros((PAD, LANES), jnp.float32)
            far[side, pl.ds(PAD + steps_out, PAD), :] = jnp.zeros((PAD, LANES), jnp.float32)

    @pl.when(step >= vblocks)
    def _():
        lane = lax.broadcasted_iota(jnp.int32, (steps_out, LANES), 1)
        for pair in range(group // 2):
            for side in range(2):
                rec = (step - vblocks) * group + pair * 2 + side
                live = live_ref[rec]
                tiles = (live + (UNROLL - 1)) // UNROLL

                def clear(i, _):
                    at = pl.ds(pl.multiple_of(PAD + i * UNROLL, UNROLL), UNROLL)
                    near[side, at, :] = jnp.zeros((UNROLL, LANES), jnp.float32)
                    far[side, at, :] = jnp.zeros((UNROLL, LANES), jnp.float32)
                    return 0

                lax.fori_loop(tiles, steps_out // UNROLL, clear, 0)

                def fetch(i, _):
                    start = rec * (2 * steps_out) + i * (2 * UNROLL)
                    for u in range(UNROLL):
                        even = ids_ref[start + 2 * u]
                        odd = ids_ref[start + 2 * u + 1]
                        at = pl.ds(PAD + i * UNROLL + u, 1)
                        near[side, at, :] = rows[0, pl.ds(even, 1), :] + rows[1, pl.ds(odd, 1), :]
                        far[side, at, :] = rows[2, pl.ds(even, 1), :]
                    return 0

                lax.fori_loop(0, tiles, fetch, 0)
            own0 = near[0, pl.ds(PAD, steps_out), :]
            own1 = near[1, pl.ds(PAD, steps_out), :]
            edge0 = near[0, pl.ds(PAD - 1, steps_out), :] + far[0, pl.ds(PAD + 1, steps_out), :]
            edge1 = near[1, pl.ds(PAD - 1, steps_out), :] + far[1, pl.ds(PAD + 1, steps_out), :]
            first = own0 + pltpu.roll(edge0, LANES // 2, 1)
            second = pltpu.roll(own1, LANES // 2, 1) + edge1
            out_ref[pair] = jnp.where(lane < LANES // 2, first, second)


def right_pairs(ids, live, table, weights, steps_out):
    vocab = table.shape[1]
    chans = table.shape[0]
    recipes = live.shape[0]
    vblk = 1280
    vblocks = vocab // vblk
    group = 4
    return pl.pallas_call(
        functools.partial(right_kernel, vocab, vblocks, group, steps_out),
        grid_spec=pltpu.PrefetchScalarGridSpec(
            num_scalar_prefetch=2,
            grid=(vblocks + recipes // group,),
            in_specs=[
                pl.BlockSpec((chans, vblk), lambda s, *_: (0, jnp.minimum(s, vblocks - 1))),
                pl.BlockSpec((chans, 3 * LANES), lambda s, *_: (0, 0)),
            ],
            out_specs=pl.BlockSpec(
                (group // 2, steps_out, LANES), lambda s, *_: (jnp.maximum(s - vblocks, 0), 0, 0)
            ),
            scratch_shapes=[
                pltpu.VMEM((3, vocab + PAD, LANES), jnp.float32),
                pltpu.VMEM((2, steps_out + 2 * PAD, LANES), jnp.float32),
                pltpu.VMEM((2, steps_out + 2 * PAD, LANES), jnp.float32),
            ],
        ),
        out_shape=jax.ShapeDtypeStruct((recipes // 2, steps_out, LANES), jnp.float32),
        compiler_params=pltpu.CompilerParams(vmem_limit_bytes=60 * 1024 * 1024),
        cost_estimate=pl.CostEstimate(
            flops=2 * vocab * chans * 3 * LANES, bytes_accessed=200 * 1024 * 1024, transcendentals=0
        ),
    )(ids, live, table, weights)


def left_part_of(lengths, cotangent, proj_a):
    steps_out = cotangent.shape[2]
    outpos = 2 * jnp.arange(steps_out, dtype=jnp.int32)
    tkeep = outpos[None, :] < lengths[:, None]
    masked = jnp.where(tkeep[:, None, :], cotangent, jnp.zeros((), cotangent.dtype))
    return jnp.einsum("nct,ca->nat", masked, proj_a, preferred_element_type=jnp.float32)


def local(token_ids, lengths, table, cotangent, proj_a, proj_b):
    recipes_here, seqlen = token_ids.shape
    chans, width = proj_a.shape
    vocab = table.shape[1]
    steps_out = seqlen // 2
    total_feats = width * width
    left_part = left_part_of(lengths, cotangent, proj_a)
    left_own = lax.psum_scatter(left_part, "tensor", scatter_dimension=0, tiled=True)

    pos = jnp.arange(seqlen, dtype=jnp.int32)
    ids = jnp.where(pos[None, :] < lengths[:, None], token_ids, vocab).reshape(-1)
    live = (lengths + 1) // 2
    tap = [proj_b[:, k, :] for k in range(5)]
    weights = jnp.concatenate([tap[2], tap[0], tap[3], tap[1], jnp.zeros_like(tap[4]), tap[4]], axis=1)
    right_part = right_pairs(ids, live, table, weights, steps_out)
    right_own = lax.psum_scatter(right_part, "tensor", scatter_dimension=0, tiled=True)
    mine = right_own.shape[0] * 2
    left_two = left_own.reshape(mine // 2, 2, width, steps_out)
    raw = jnp.stack(
        [
            jnp.einsum(
                "nat,ntb->nab", left_two[:, side], right_own[:, :, side * width:(side + 1) * width],
                precision=lax.Precision.HIGHEST,
            )
            for side in range(2)
        ],
        axis=1,
    ).reshape(mine, total_feats)
    scale = lax.rsqrt(jnp.mean(raw * raw, axis=1) + 1e-06)
    unit = (raw * scale[:, None]).astype(jnp.bfloat16)
    every = lax.all_gather(unit, ("dp", "tensor"), axis=0, tiled=True)
    terms = lax.dot_general(
        unit, every, (((1,), (1,)), ((), ())), preferred_element_type=jnp.float32
    )
    return terms * (1.0 / total_feats)


def solution(mesh):
    placed = (
        P("dp", None),
        P("dp"),
        P("tensor", None),
        P("dp", "tensor", None),
        P("tensor", None),
        P("tensor", None, None),
    )
    return jax.shard_map(
        local, mesh=mesh, in_specs=placed, out_specs=P(("dp", "tensor"), None), check_vma=False
    )
```

time: 508 us -> 194 us (0.38)
  local copies, waits for them, and re-layouts: 225 us -> 3.8 us
  other arithmetic: 87.7 us -> 3.03 us
  Pallas kernels: 0 us -> 44.1 us
  blocking collectives: 37.7 us -> 0 us
  matrix products: 35.9 us -> 10.5 us
  waiting for transfers between devices: 106 us -> 119 us
    gather x4 -> x0, local copies, waits for them, and re-layouts: 141 us -> none  [right_block(): rows = jnp.take(projected, ids_b.reshape(count * seqlen), axis=0)]
    mul x5 -> x1, other arithmetic: 51.3 us -> 0.01 us  [left_part_of(): outpos = 2 * jnp.arange(steps_out, dtype=jnp.int32)]
    slice x6 -> x1, local copies, waits for them, and re-layouts: 49.3 us -> 0.83 us  [local(): tap = [proj_b[:, k, :] for k in range(5)]]
    pallas_call x0 -> x1, Pallas kernels: none -> 44.1 us  [right_pairs(): pl.pallas_call(functools.partial(right_kernel, vocab, vblocks, group, ste...]
    all_gather x1, waiting for transfers between devices: 24.2 us -> 56.5 us  [local(): every = lax.all_gather(unit, ('dp', 'tensor'), axis=0, tiled=True)]
    all_gather x1 -> x0, blocking collectives: 31.8 us -> none  [local(): lax.all_gather(panel_flat, 'dp', axis=0, tiled=True)]
    add x2 -> x0, other arithmetic: 30.5 us -> none  [right_block(): before = even[:, :, 0] + odd[:, :, 1]]
    dot_general x5 -> x4, matrix products: 35.9 us -> 10.5 us  [the longest x1 4.35 us: left_part_of(): jnp.einsum('nct,ca->nat', masked, proj_a, preferred_element_type=jnp.floa...]
  transfers between devices with their start and end apart: 4 -> 3, of which waited for: 4 -> 3; matrix products, arithmetic and copies ran while one was open for 1% -> 2% of each run, Pallas kernels for 0% -> 0%
where the time goes in v1:
time: 194 us
  waiting for transfers between devices  119 us (61%)
  Pallas kernels  44.1 us (23%)
  between operations  13.2 us (7%)
  matrix products  10.5 us (5%)
  local copies, waits for them, and re-layouts  3.8 us (2%)
  other arithmetic  3.03 us (2%)
    all_gather x1, waiting for transfers between devices, local(): every = lax.all_gather(unit, ('dp', 'tensor'), axis=0, tiled=True)  56.5 us
    pallas_call x1, Pallas kernels, right_pairs(): pl.pallas_call(functools.partial(right_kernel, vocab, vblocks, group, ste...  44.1 us
    reduce_scatter x1, waiting for transfers between devices, local(): lax.psum_scatter(left_part, 'tensor', scatter_dimension=0, tiled=True)  34.2 us
    reduce_scatter x1, waiting for transfers between devices, local(): lax.psum_scatter(right_part, 'tensor', scatter_dimension=0, tiled=True)  28.3 us
    dot_general x1, matrix products, left_part_of(): jnp.einsum('nct,ca->nat', masked, proj_a, preferred_element_type=jnp.floa...  4.35 us
  transfers between devices with their start and end apart: 3, of which 3 were waited for; matrix products, arithmetic and copies ran while one was open for 2% of the time, Pallas kernels for 0%

profile of v1, /device:TPU:0, one launch (start us, length us, event | category | flops | bytes accessed | tf_op | source)
XLA Modules:
  0.0 193.7 jit_solution(16348122908674243355)
XLA Ops:
  6.5 0.0 copy-start
  6.5 0.0 reduce-scatter.5.cloned.1.call-start
  6.5 1.2 and_select_fusion.live_ref
  7.7 0.9 select_bitcast_fusion
  8.6 0.6 copy.46
  9.3 0.8 fusion.11
  10.1 0.1 copy.44
  10.2 0.1 copy.43
  10.3 0.1 copy.42
  10.5 0.1 copy.41
  10.6 0.1 copy.40
  10.7 0.8 concatenate.3.w_ref
  11.6 44.1 %shard_map.64 = f32[16,256,128]{2,1,0:T(8,128)} custom-call(s32[16384]{0:T(1024)} %bitcast.39, s32[32]{0:T(128)} %and_select_fusion.live_ref, bf16[256,32000]{1,0:T(8,128)(2,1)} %table_ref.1, bf16[256,384]{1,0:T(8,128)(2,1)} %concatenate.3.w_ref), custom_call_target="tpu_custom_call" | custom-call | flops 6291456000 | bytes 209715200 | tf_op jit(solution)/shard_map/pallas_call | solution.py:80
  55.7 0.0 copy-start.1
  55.7 0.0 reduce-scatter.5.cloned.1.call-update
  55.7 0.0 reduce-scatter.3.cloned.1.call-start
  55.8 0.6 copy-done.1
  56.4 0.1 broadcast_compare_fusion
  56.4 0.0 copy-done
  56.4 4.3 %fusion.4 = f32[32,64,256]{2,1,0:T(8,128)} fusion(bf16[32,256,256]{2,1,0:T(8,128)(2,1)} %param.9, pred[32,256]{1,0:T(8,128)(4,1)S(1)} %broadcast_compare_fusion, bf16[256,64]{0,1:T(8,128)(2,1)S(1)} %copy-done), kind=kOutput, calls=%fused_computation.4 | convolution fusion | flops 270532608 | bytes 6332416 | tf_op jit(solution)/shard_map/nct,ca->nat/dot_general | solution.py:111
  60.8 0.0 reduce-scatter.3.cloned.1.call-update
  60.8 0.0 all-gather.2.cloned.1.call-start
  60.9 28.3 %reduce-scatter.5.cloned.1.call-done = f32[4,256,128]{2,1,0:T(8,128)} async-done(((f32[16,256,128]{2,1,0:T(8,128)}), f32[4,256,128]{2,1,0:T(8,128)}) %reduce-scatter.5.cloned.1.call-update) | async-done | bytes 524304 | tf_op jit(solution)/shard_map/reduce_scatter | solution.py:129
  89.2 34.2 %reduce-scatter.3.cloned.1.call-done = f32[8,64,256]{2,1,0:T(8,128)} async-done(((f32[32,64,256]{2,1,0:T(8,128)}), f32[8,64,256]{2,1,0:T(8,128)}) %reduce-scatter.3.cloned.1.call-update) | async-done | bytes 524304 | tf_op jit(solution)/shard_map/reduce_scatter | solution.py:121
  123.3 1.6 convolution_bitcast_fusion.1
  124.9 1.7 convolution_bitcast_fusion
  126.6 0.1 multiply_reduce_fusion
  126.7 0.1 copy.36
  126.8 0.1 rsqrt.11
  127.0 0.1 reshape.52
  127.1 0.7 multiply_convert_fusion
  127.8 0.0 all-gather.2.cloned.1.call-update
  127.8 56.5 %all-gather.2.cloned.1.call-done = bf16[256,4096]{1,0:T(8,128)(2,1)} async-done(((bf16[8,4096]{1,0:T(8,128)(2,1)}), bf16[256,4096]{1,0:T(8,128)(2,1)}) %all-gather.2.cloned.1.call-update) | async-done | bytes 2097168 | tf_op jit(solution)/shard_map/all_gather | solution.py:144
  184.3 2.9 %convolution_multiply_fusion = f32[8,256]{1,0:T(8,128)} fusion(bf16[8,4096]{1,0:T(8,128)(2,1)} %multiply_convert_fusion, bf16[256,4096]{1,0:T(8,128)(2,1)} %all-gather.2.cloned.1.call-done), kind=kOutput, calls=%fused_computation.7 | convolution fusion | flops 16779264 | bytes 2170880 | tf_op jit(solution)/shard_map/dot_general | solution.py:145
  (4 shorter events, 0.0 us)
Async XLA Ops:
  6.5 49.9 %copy-start = (bf16[256,64]{0,1:T(8,128)(2,1)S(1)}, bf16[256,64]{0,1:T(8,128)(2,1)}, u32[]{:S(2)}) copy-start(bf16[256,64]{0,1:T(8,128)(2,1)} %param.10) | copy-start | bytes 98308
  6.5 82.6 %reduce-scatter.5.cloned.1.call-start = ((), (), s32[]{:S(2)}) async-start(), calls=%async_computation.3 | async-start | bytes 2621440 | tf_op jit(solution)/shard_map/reduce_scatter | solution.py:129
  55.7 0.7 copy-start.1
  55.7 67.6 %reduce-scatter.3.cloned.1.call-start = ((), (), s32[]{:S(2)}) async-start(), calls=%async_computation.2 | async-start | bytes 2621440 | tf_op jit(solution)/shard_map/reduce_scatter | solution.py:121
  60.8 123.5 %all-gather.2.cloned.1.call-start = ((), (), s32[]{:S(2)}) async-start(), calls=%async_computation.4 | async-start | bytes 2162688 | tf_op jit(solution)/shard_map/all_gather | solution.py:144
Sparse Core Ops, SparseCore 0:
  55.9 33.2 reduce-scatter.4
  91.9 31.4 reduce-scatter.2
  127.9 56.3 all-gather.1

commit v2 on v1

--- a/solution.py
+++ b/solution.py
@@ -103,6 +103,148 @@
     )(ids, live, table, weights)
 
 
+def share_kernel(dp_count, left_ref, part_ref, out_ref, core_in, core_own, cross_out, cross_in,
+                 planes, packed, every, sums, got, core_send, core_recv, cross_send, cross_recv,
+                 slice_send, slice_recv, wide_send, wide_recv, row_send, row_recv):
+    me = lax.axis_index("tensor")
+    block = lax.axis_index("dp")
+    sib = me + 1 - 2 * (me % 2)
+    across = (me + 2) % 4
+    diag = (sib + 2) % 4
+    pairs = left_ref.shape[0]
+    half = LANES // 2
+    feats = half * half
+    mesh_ids = pl.DeviceIdType.MESH
+
+    barrier = pltpu.get_barrier_semaphore()
+    for off in range(1, 4):
+        pl.semaphore_signal(barrier, inc=1, device_id={"tensor": (me + off) % 4}, device_id_type=mesh_ids)
+    for off in range(1, dp_count):
+        pl.semaphore_signal(barrier, inc=1, device_id={"dp": (block + off) % dp_count}, device_id_type=mesh_ids)
+    pl.semaphore_wait(barrier, 3 + dp_count - 1)
+
+    def remote(src, dst, send, recv, where):
+        return pltpu.make_async_remote_copy(
+            src_ref=src, dst_ref=dst, send_sem=send, recv_sem=recv, device_id=where, device_id_type=mesh_ids
+        )
+
+    first = [
+        remote(part_ref.at[diag * pairs + i], core_in.at[i], core_send.at[i], core_recv.at[i], {"tensor": sib})
+        for i in range(pairs)
+    ]
+    second = [
+        remote(part_ref.at[sib * pairs + i], core_own.at[i], core_send.at[pairs + i], core_recv.at[pairs + i],
+               {"tensor": sib})
+        for i in range(pairs)
+    ]
+    for copy in first + second:
+        copy.start()
+    over = [
+        remote(cross_out.at[i], cross_in.at[i], cross_send.at[i], cross_recv.at[i], {"tensor": across})
+        for i in range(pairs)
+    ]
+    for i in range(pairs):
+        first[i].wait_recv()
+        cross_out[i] = (part_ref[across * pairs + i] + core_in[i]).astype(jnp.bfloat16)
+        over[i].start()
+
+    lane = lax.broadcasted_iota(jnp.int32, (half // 2, LANES), 1) < half
+    quarter = half // 2
+    for i in range(pairs):
+        second[i].wait_recv()
+        mine = part_ref[me * pairs + i] + core_own[i]
+        over[i].wait_recv()
+        right = mine + cross_in[i].astype(jnp.float32)
+        raw = lax.dot_general(
+            left_ref[i], right, (((1,), (0,)), ((), ())),
+            precision=lax.Precision.HIGHEST, preferred_element_type=jnp.float32,
+        )
+        top = jnp.where(lane, raw[:quarter], pltpu.roll(raw[quarter:half], half, 1))
+        low = jnp.where(lane, pltpu.roll(raw[half:half + quarter], half, 1), raw[half + quarter:])
+        for side, vals in enumerate((top, low)):
+            total = jnp.sum(jnp.sum(vals * vals, axis=0, keepdims=True), axis=1, keepdims=True)
+            planes[:, 2 * i + side, :] = vals * lax.rsqrt(total / feats + 1e-06)
+
+    depth = packed.shape[1]
+    for j in range(4):
+        packed[j] = planes[j * depth:(j + 1) * depth].astype(jnp.bfloat16)
+    every[block, me] = packed[me]
+    slices = []
+    for off in range(1, 4):
+        peer = (me + off) % 4
+        slices.append(
+            remote(packed.at[peer], every.at[block, me], slice_send.at[off - 1], slice_recv.at[off - 1],
+                   {"tensor": peer})
+        )
+    for copy in slices:
+        copy.start()
+    for copy in slices:
+        copy.wait_recv()
+    wide = [
+        remote(every.at[block], every.at[block], wide_send.at[off - 1], wide_recv.at[off - 1],
+               {"dp": (block + off) % dp_count})
+        for off in range(1, dp_count)
+    ]
+    for copy in wide:
+        copy.start()
+    for copy in wide:
+        copy.wait_recv()
+
+    recs = packed.shape[2]
+    total = jnp.zeros((4 * recs, dp_count * 4 * recs), jnp.float32)
+    for plane in range(depth):
+        lhs = every[block, :, plane].astype(jnp.float32).reshape(4 * recs, LANES).astype(jnp.bfloat16)
+        rhs = every[:, :, plane].astype(jnp.float32).reshape(dp_count * 4 * recs, LANES).astype(jnp.bfloat16)
+        total += lax.dot_general(lhs, rhs, (((1,), (1,)), ((), ())), preferred_element_type=jnp.float32)
+    for j in range(4):
+        sums[j] = total[j * recs:(j + 1) * recs]
+    rows = []
+    for off in range(1, 4):
+        peer = (me + off) % 4
+        rows.append(
+            remote(sums.at[peer], got.at[off - 1], row_send.at[off - 1], row_recv.at[off - 1], {"tensor": peer})
+        )
+    for copy in rows:
+        copy.start()
+    result = sums[me]
+    for off in range(3):
+        rows[off].wait_recv()
+        result = result + got[off]
+    out_ref[...] = result
+    for copy in first + second + over + slices + wide + rows:
+        copy.wait_send()
+
+
+def share(left_two, right_part, dp_count):
+    pairs, _, steps_out = left_two.shape
+    recs = 2 * pairs
+    depth = LANES // 16
+    vmem = pl.BlockSpec(memory_space=pltpu.VMEM)
+    dma = pltpu.SemaphoreType.DMA
+    return pl.pallas_call(
+        functools.partial(share_kernel, dp_count),
+        out_shape=jax.ShapeDtypeStruct((recs, dp_count * 4 * recs), jnp.float32),
+        in_specs=[vmem, vmem],
+        out_specs=vmem,
+        scratch_shapes=[
+            pltpu.VMEM((pairs, steps_out, LANES), jnp.float32),
+            pltpu.VMEM((pairs, steps_out, LANES), jnp.float32),
+            pltpu.VMEM((pairs, steps_out, LANES), jnp.bfloat16),
+            pltpu.VMEM((pairs, steps_out, LANES), jnp.bfloat16),
+            pltpu.VMEM((4 * depth, recs, LANES), jnp.float32),
+            pltpu.VMEM((4, depth, recs, LANES), jnp.bfloat16),
+            pltpu.VMEM((dp_count, 4, depth, recs, LANES), jnp.bfloat16),
+            pltpu.VMEM((4, recs, dp_count * 4 * recs), jnp.float32),
+            pltpu.VMEM((3, recs, dp_count * 4 * recs), jnp.float32),
+            dma((2 * pairs,)), dma((2 * pairs,)), dma((pairs,)), dma((pairs,)),
+            dma((3,)), dma((3,)), dma((dp_count - 1,)), dma((dp_count - 1,)), dma((3,)), dma((3,)),
+        ],
+        compiler_params=pltpu.CompilerParams(
+            collective_id=0, has_side_effects=True, vmem_limit_bytes=40 * 1024 * 1024
+        ),
+    )(left_two, right_part)
+
+
 def left_part_of(lengths, cotangent, proj_a):
     steps_out = cotangent.shape[2]
     outpos = 2 * jnp.arange(steps_out, dtype=jnp.int32)
@@ -118,14 +260,19 @@
     steps_out = seqlen // 2
     total_feats = width * width
     left_part = left_part_of(lengths, cotangent, proj_a)
-    left_own = lax.psum_scatter(left_part, "tensor", scatter_dimension=0, tiled=True)
 
     pos = jnp.arange(seqlen, dtype=jnp.int32)
     ids = jnp.where(pos[None, :] < lengths[:, None], token_ids, vocab).reshape(-1)
     live = (lengths + 1) // 2
     tap = [proj_b[:, k, :] for k in range(5)]
     weights = jnp.concatenate([tap[2], tap[0], tap[3], tap[1], jnp.zeros_like(tap[4]), tap[4]], axis=1)
+    weights, left_part = lax.optimization_barrier((weights, left_part))
+    left_own = lax.psum_scatter(left_part, "tensor", scatter_dimension=0, tiled=True)
     right_part = right_pairs(ids, live, table, weights, steps_out)
+    if lax.axis_size("tensor") == 4:
+        mine = left_own.shape[0]
+        paired = left_own.reshape(mine // 2, 2 * width, steps_out)
+        return share(paired, right_part, lax.axis_size("dp")) * (1.0 / total_feats)
     right_own = lax.psum_scatter(right_part, "tensor", scatter_dimension=0, tiled=True)
     mine = right_own.shape[0] * 2
     left_two = left_own.reshape(mine // 2, 2, width, steps_out)

time: 194 us -> 102 us (0.53)
  the two profiles are of different devices: /device:TPU:0 before, /device:TPU:13 now
where the time goes in v2:
time: 102 us; the launch traced here: 101 us
  Pallas kernels  75.7 us (74%)
  between operations  13.5 us (13%)
  local copies, waits for them, and re-layouts  5.57 us (5%)
  matrix products  4.42 us (4%)
  other arithmetic  1.93 us (2%)
    pallas_call x1, Pallas kernels, right_pairs(): pl.pallas_call(functools.partial(right_kernel, vocab, vblocks, group, ste...  43 us
    pallas_call x1, Pallas kernels, share(): pl.pallas_call(functools.partial(share_kernel, dp_count), out_shape=jax.S...  32.7 us
    dot_general x1, matrix products, left_part_of(): jnp.einsum('nct,ca->nat', masked, proj_a, preferred_element_type=jnp.floa...  4.42 us
    unnamed x16, local copies, waits for them, and re-layouts  3.89 us
  transfers between devices with their start and end apart: 1, of which 0 were waited for; matrix products, arithmetic and copies ran while one was open for 1% of the time, Pallas kernels for 43%

profile of v2, /device:TPU:13, one launch (start us, length us, event | category | flops | bytes accessed | tf_op | source)
XLA Modules:
  0.0 101.1 jit_solution(6937938229461632979)
XLA Ops:
  6.5 0.0 copy-start
  6.5 0.0 reduce-scatter.2.cloned.1.call-start
  6.5 0.8 fusion.9
  7.4 0.1 copy.12
  7.5 0.1 copy.13
  7.6 0.1 copy.14
  7.8 0.1 copy.15
  7.9 0.1 copy.16
  8.0 0.7 broadcast_compare_fusion
  8.7 0.0 copy-done
  8.7 0.0 copy-start.3
  8.8 0.0 copy-start.4
  8.8 4.4 %fusion.4 = f32[32,64,256]{2,1,0:T(8,128)} fusion(bf16[32,256,256]{2,1,0:T(8,128)(2,1)} %param.9, pred[32,256]{1,0:T(8,128)(4,1)S(1)} %broadcast_compare_fusion, bf16[256,64]{0,1:T(8,128)(2,1)S(1)} %copy-done), kind=kOutput, calls=%fused_computation.4 | convolution fusion | flops 270532608 | bytes 6332416 | tf_op jit(solution)/shard_map/nct,ca->nat/dot_general | solution.py:253
  13.2 0.8 concatenate.3.w_ref
  14.0 0.0 reduce-scatter.2.cloned.1.call-update
  14.1 0.0 copy-done.3
  14.1 0.0 copy-done.4
  14.1 0.1 select_bitcast_fusion
  14.2 0.7 copy.17
  14.8 0.5 and_select_fusion.live_ref
  15.3 43.0 %shard_map.64.part_ref = f32[16,256,128]{2,1,0:T(8,128)} custom-call(s32[16384]{0:T(1024)} %bitcast.20, s32[32]{0:T(128)} %and_select_fusion.live_ref, bf16[256,32000]{1,0:T(8,128)(2,1)} %table_ref.1, bf16[256,384]{1,0:T(8,128)(2,1)} %concatenate.3.w_ref), custom_call_target="tpu_custom_call" | custom-call | flops 6291456000 | bytes 209715200 | tf_op jit(solution)/shard_map/pallas_call | solution.py:80
  58.3 0.0 reduce-scatter.2.cloned.1.call-done
  58.3 0.0 copy-start.1
  58.3 1.6 %copy-done.1 = f32[16,256,128]{2,1,0:T(8,128)S(1)} copy-done((f32[16,256,128]{2,1,0:T(8,128)S(1)}, f32[16,256,128]{2,1,0:T(8,128)}, u32[]{:S(2)}) %copy-start.1) | copy-done | bytes 2097176
  59.9 0.0 copy-start.2
  59.9 1.0 %copy-done.2 = f32[8,64,256]{2,1,0:T(8,128)S(1)} copy-done((f32[8,64,256]{2,1,0:T(8,128)S(1)}, f32[8,64,256]{2,1,0:T(8,128)}, u32[]{:S(2)}) %copy-start.2) | copy-done | bytes 524312
  60.9 32.7 %shard_map.65 = f32[8,256]{1,0:T(8,128)S(1)} custom-call(f32[4,128,256]{2,1,0:T(8,128)S(1)} %bitcast.14, f32[16,256,128]{2,1,0:T(8,128)S(1)} %copy-done.1), custom_call_target="tpu_custom_call" | custom-call | tf_op jit(solution)/shard_map/pallas_call | solution.py:224
  93.7 0.6 broadcast_multiply_fusion
  (2 shorter events, 0.0 us)
Async XLA Ops:
  6.5 2.2 %copy-start = (bf16[256,64]{0,1:T(8,128)(2,1)S(1)}, bf16[256,64]{0,1:T(8,128)(2,1)}, u32[]{:S(2)}) copy-start(bf16[256,64]{0,1:T(8,128)(2,1)} %param.10) | copy-start | bytes 98308
  6.5 51.8 %reduce-scatter.2.cloned.1.call-start = ((), (), s32[]{:S(2)}) async-start(), calls=%async_computation.1 | async-start | bytes 2621440 | tf_op jit(solution)/shard_map/reduce_scatter | solution.py:270
  8.7 5.3 %copy-start.3 = (s32[32,512]{1,0:T(8,128)S(1)}, s32[32,512]{1,0:T(8,128)}, u32[]{:S(2)}) copy-start(s32[32,512]{1,0:T(8,128)} %param.6) | copy-start | bytes 196612
  8.8 5.3 %copy-start.4 = (s32[32]{0:T(128)S(1)}, s32[32]{0:T(128)}, u32[]{:S(2)}) copy-start(s32[32]{0:T(128)} %param.7) | copy-start | bytes 388
  58.3 1.6 %copy-start.1 = (f32[16,256,128]{2,1,0:T(8,128)S(1)}, f32[16,256,128]{2,1,0:T(8,128)}, u32[]{:S(2)}) copy-start(f32[16,256,128]{2,1,0:T(8,128)} %shard_map.64.part_ref) | copy-start | bytes 6291460
  59.9 1.0 %copy-start.2 = (f32[8,64,256]{2,1,0:T(8,128)S(1)}, f32[8,64,256]{2,1,0:T(8,128)}, u32[]{:S(2)}) copy-start(f32[8,64,256]{2,1,0:T(8,128)} %reduce-scatter.2.cloned.1.call-done) | copy-start | bytes 1572868
Sparse Core Ops, SparseCore 0:
  14.2 32.5 reduce-scatter.1

commit v3 on v2

--- a/solution.py
+++ b/solution.py
@@ -10,20 +10,32 @@
 LANES = 128
 UNROLL = 8
 PAD = 8
-
-
-def right_kernel(vocab, vblocks, group, steps_out, ids_ref, live_ref, table_ref, w_ref, out_ref, rows, near, far):
+CHUNK = 640
+
+
+def right_kernel(vocab, vblocks, group, steps_out, ids_ref, live_ref, table_ref, w_ref, out_ref, rows, near, far, wts):
     step = pl.program_id(0)
     vblk = table_ref.shape[1]
 
+    @pl.when(step == 0)
+    def _():
+        tap = [w_ref[k] for k in range(5)]
+        wts[...] = jnp.concatenate([tap[2], tap[0], tap[3], tap[1], jnp.zeros_like(tap[4]), tap[4]], axis=0)
+
     @pl.when(step < vblocks)
     def _():
-        base = pl.multiple_of(step * vblk, LANES)
-        part = lax.dot_general(
-            table_ref[...], w_ref[...], (((0,), (0,)), ((), ())), preferred_element_type=jnp.float32
-        )
-        for col in range(3):
-            rows[col, pl.ds(base, vblk), :] = part[:, col * LANES:(col + 1) * LANES]
+        def project(i, _):
+            at = pl.multiple_of(i * CHUNK, LANES)
+            base = pl.multiple_of(step * vblk + at, LANES)
+            part = lax.dot_general(
+                table_ref[:, pl.ds(at, CHUNK)], wts[...], (((0,), (1,)), ((), ())),
+                preferred_element_type=jnp.float32,
+            )
+            for col in range(3):
+                rows[col, pl.ds(base, CHUNK), :] = part[:, col * LANES:(col + 1) * LANES]
+            return 0
+
+        lax.fori_loop(0, vblk // CHUNK, project, 0, unroll=True)
 
     @pl.when(step == vblocks)
     def _():
@@ -51,10 +63,10 @@
                 lax.fori_loop(tiles, steps_out // UNROLL, clear, 0)
 
                 def fetch(i, _):
-                    start = rec * (2 * steps_out) + i * (2 * UNROLL)
+                    start = i * (2 * UNROLL)
                     for u in range(UNROLL):
-                        even = ids_ref[start + 2 * u]
-                        odd = ids_ref[start + 2 * u + 1]
+                        even = ids_ref[rec, start + 2 * u]
+                        odd = ids_ref[rec, start + 2 * u + 1]
                         at = pl.ds(PAD + i * UNROLL + u, 1)
                         near[side, at, :] = rows[0, pl.ds(even, 1), :] + rows[1, pl.ds(odd, 1), :]
                         far[side, at, :] = rows[2, pl.ds(even, 1), :]
@@ -74,7 +86,7 @@
     vocab = table.shape[1]
     chans = table.shape[0]
     recipes = live.shape[0]
-    vblk = 1280
+    vblk = 5 * CHUNK
     vblocks = vocab // vblk
     group = 4
     return pl.pallas_call(
@@ -84,7 +96,7 @@
             grid=(vblocks + recipes // group,),
             in_specs=[
                 pl.BlockSpec((chans, vblk), lambda s, *_: (0, jnp.minimum(s, vblocks - 1))),
-                pl.BlockSpec((chans, 3 * LANES), lambda s, *_: (0, 0)),
+                pl.BlockSpec(weights.shape, lambda s, *_: (0, 0, 0)),
             ],
             out_specs=pl.BlockSpec(
                 (group // 2, steps_out, LANES), lambda s, *_: (jnp.maximum(s - vblocks, 0), 0, 0)
@@ -93,6 +105,7 @@
                 pltpu.VMEM((3, vocab + PAD, LANES), jnp.float32),
                 pltpu.VMEM((2, steps_out + 2 * PAD, LANES), jnp.float32),
                 pltpu.VMEM((2, steps_out + 2 * PAD, LANES), jnp.float32),
+                pltpu.VMEM((3 * LANES, chans), jnp.bfloat16),
             ],
         ),
         out_shape=jax.ShapeDtypeStruct((recipes // 2, steps_out, LANES), jnp.float32),
@@ -103,7 +116,7 @@
     )(ids, live, table, weights)
 
 
-def share_kernel(dp_count, left_ref, part_ref, out_ref, core_in, core_own, cross_out, cross_in,
+def share_kernel(dp_count, left_ref, left_b, left_c, left_d, part_ref, out_ref, core_in, core_own, cross_out, cross_in,
                  planes, packed, every, sums, got, core_send, core_recv, cross_send, cross_recv,
                  slice_send, slice_recv, wide_send, wide_recv, row_send, row_recv):
     me = lax.axis_index("tensor")
@@ -156,7 +169,7 @@
         over[i].wait_recv()
         right = mine + cross_in[i].astype(jnp.float32)
         raw = lax.dot_general(
-            left_ref[i], right, (((1,), (0,)), ((), ())),
+            (left_ref[i] + left_b[i]) + (left_c[i] + left_d[i]), right, (((1,), (0,)), ((), ())),
             precision=lax.Precision.HIGHEST, preferred_element_type=jnp.float32,
         )
         top = jnp.where(lane, raw[:quarter], pltpu.roll(raw[quarter:half], half, 1))
@@ -215,8 +228,8 @@
         copy.wait_send()
 
 
-def share(left_two, right_part, dp_count):
-    pairs, _, steps_out = left_two.shape
+def share(lefts, right_part, dp_count):
+    pairs, _, steps_out = lefts[0].shape
     recs = 2 * pairs
     depth = LANES // 16
     vmem = pl.BlockSpec(memory_space=pltpu.VMEM)
@@ -224,7 +237,7 @@
     return pl.pallas_call(
         functools.partial(share_kernel, dp_count),
         out_shape=jax.ShapeDtypeStruct((recs, dp_count * 4 * recs), jnp.float32),
-        in_specs=[vmem, vmem],
+        in_specs=[vmem] * 5,
         out_specs=vmem,
         scratch_shapes=[
             pltpu.VMEM((pairs, steps_out, LANES), jnp.float32),
@@ -242,7 +255,7 @@
         compiler_params=pltpu.CompilerParams(
             collective_id=0, has_side_effects=True, vmem_limit_bytes=40 * 1024 * 1024
         ),
-    )(left_two, right_part)
+    )(*lefts, right_part)
 
 
 def left_part_of(lengths, cotangent, proj_a):
@@ -262,17 +275,26 @@
     left_part = left_part_of(lengths, cotangent, proj_a)
 
     pos = jnp.arange(seqlen, dtype=jnp.int32)
-    ids = jnp.where(pos[None, :] < lengths[:, None], token_ids, vocab).reshape(-1)
+    ids = jnp.where(pos[None, :] < lengths[:, None], token_ids, vocab)
     live = (lengths + 1) // 2
-    tap = [proj_b[:, k, :] for k in range(5)]
-    weights = jnp.concatenate([tap[2], tap[0], tap[3], tap[1], jnp.zeros_like(tap[4]), tap[4]], axis=1)
-    weights, left_part = lax.optimization_barrier((weights, left_part))
+    weights = jnp.transpose(proj_b, (1, 2, 0))
+    if lax.axis_size("tensor") == 4:
+        mine = recipes_here // 4
+        me = lax.axis_index("tensor")
+        pieces = left_part.reshape(4, mine // 2, 2 * width, steps_out)
+        partners = [[j + 1 - 2 * (j % 2) for j in range(4)], [(j + 2) % 4 for j in range(4)]]
+        partners.append([(j + 2) % 4 for j in partners[0]])
+        offsets = [1 - 2 * (me % 2), 2, 3 - 2 * (me % 2)]
+        own = lax.dynamic_index_in_dim(pieces, me, 0, keepdims=False)
+        gifts = [lax.dynamic_index_in_dim(pieces, (me + off) % 4, 0, keepdims=False) for off in offsets]
+        weights, *gifts = lax.optimization_barrier((weights, *gifts))
+        lefts = [own] + [
+            lax.ppermute(gift, "tensor", list(enumerate(to))) for gift, to in zip(gifts, partners)
+        ]
+        right_part = right_pairs(ids, live, table, weights, steps_out)
+        return share(lefts, right_part, lax.axis_size("dp")) * (1.0 / total_feats)
     left_own = lax.psum_scatter(left_part, "tensor", scatter_dimension=0, tiled=True)
     right_part = right_pairs(ids, live, table, weights, steps_out)
-    if lax.axis_size("tensor") == 4:
-        mine = left_own.shape[0]
-        paired = left_own.reshape(mine // 2, 2 * width, steps_out)
-        return share(paired, right_part, lax.axis_size("dp")) * (1.0 / total_feats)
     right_own = lax.psum_scatter(right_part, "tensor", scatter_dimension=0, tiled=True)
     mine = right_own.shape[0] * 2
     left_two = left_own.reshape(mine // 2, 2, width, steps_out)

time: 102 us -> 95.1 us (0.932)
  the two profiles are of different devices: /device:TPU:13 before, /device:TPU:0 now
where the time goes in v3:
time: 95.1 us; the launch traced here: 93.8 us
  Pallas kernels  83.1 us (87%)
  starting transfers between devices  3.15 us (3%)
  matrix products  3.07 us (3%)
  other arithmetic  2.55 us (3%)
  local copies, waits for them, and re-layouts  1.82 us (2%)
    pallas_call x1, Pallas kernels, right_pairs(): pl.pallas_call(functools.partial(right_kernel, vocab, vblocks, group, ste...  51.5 us
    pallas_call x1, Pallas kernels, share(): pl.pallas_call(functools.partial(share_kernel, dp_count), out_shape=jax.S...  31.6 us
    ppermute x3, starting transfers between devices, local(): lax.ppermute(gift, 'tensor', list(enumerate(to)))  3.15 us
    dot_general x1, matrix products, left_part_of(): jnp.einsum('nct,ca->nat', masked, proj_a, preferred_element_type=jnp.floa...  3.07 us
  transfers between devices with their start and end apart: 3, of which 0 were waited for; matrix products, arithmetic and copies ran while one was open for 1% of the time, Pallas kernels for 55%

profile of v3, /device:TPU:0, one launch (start us, length us, event | category | flops | bytes accessed | tf_op | source)
XLA Modules:
  0.0 93.8 jit_solution(7809567243867566766)
XLA Ops:
  0.0 0.0 copy-start
  0.0 0.7 broadcast_compare_fusion
  0.7 0.0 copy-done
  0.8 0.0 copy-start.3
  0.8 0.0 copy-start.2
  0.8 3.1 %fusion = f32[32,256,64]{1,2,0:T(8,128)S(1)} fusion(bf16[32,256,256]{2,1,0:T(8,128)(2,1)} %param.9, pred[32,256]{1,0:T(8,128)(4,1)S(1)} %broadcast_compare_fusion, bf16[256,64]{0,1:T(8,128)(2,1)S(1)} %copy-done), kind=kOutput, calls=%fused_computation | convolution fusion | flops 270532608 | bytes 6332416 | tf_op jit(solution)/shard_map/nct,ca->nat/dot_general | solution.py:266
  3.9 0.2 dynamic-slice_bitcast_fusion
  4.1 0.5 collective-permute-start
  4.6 2.6 %collective-permute-start.1 = (f32[4,128,256]{2,1,0:T(8,128)S(1)}, f32[4,128,256]{2,1,0:T(8,128)S(1)}, u32[]{:S(2)}, u32[]{:S(2)}) collective-permute-start(f32[4,128,256]{2,1,0:T(8,128)S(1)} %get-tuple-element.10), channel_id=1, source_target_pairs={{0,2},{1,3},{2,0},{3,1},{4,6},{5,7},{6,4},{7,5},{8,10},{9,11},{10,... | collective-permute-start | bytes 1572872 | tf_op jit(solution)/shard_map/ppermute | solution.py:292
  7.2 0.1 collective-permute-start.2
  7.2 0.0 copy-done.3
  7.2 0.5 and_select_fusion.live_ref
  7.7 0.0 copy-done.2
  7.7 0.7 fusion.4.ids_ref
  8.4 51.5 %shard_map.64.part_ref = f32[16,256,128]{2,1,0:T(8,128)} custom-call(s32[32,512]{1,0:T(8,128)} %fusion.4.ids_ref, s32[32]{0:T(128)} %and_select_fusion.live_ref, bf16[256,32000]{1,0:T(8,128)(2,1)} %table_ref.1, bf16[5,64,256]{2,1,0:T(8,128)(2,1)} %bitcast.16), custom_call_target="tpu_custom_call" | custom-call | flops 6291456000 | bytes 209715200 | tf_op jit(solution)/shard_map/pallas_call | solution.py:92
  59.9 0.0 collective-permute-done.left_b
  59.9 0.0 collective-permute-done.1.left_c
  59.9 0.0 collective-permute-done.2.left_d
  59.9 0.0 copy-start.1
  60.0 1.6 %copy-done.1 = f32[16,256,128]{2,1,0:T(8,128)S(1)} copy-done((f32[16,256,128]{2,1,0:T(8,128)S(1)}, f32[16,256,128]{2,1,0:T(8,128)}, u32[]{:S(2)}) %copy-start.1) | copy-done | bytes 2097176
  61.5 31.6 %shard_map.65 = f32[8,256]{1,0:T(8,128)S(1)} custom-call(f32[4,128,256]{2,1,0:T(8,128)S(1)} %get-tuple-element.16.left_ref, f32[4,128,256]{2,1,0:T(8,128)S(1)} %collective-permute-done.left_b, f32[4,128,256]{2,1,0:T(8,128)S(1)} %collective-permute-done.1.left_c, f32[4,128,256]{2,1,0:T(8,128)S(1)} %collective-permute-done.2.left_d, f32[16,256,128]{2,1,0:T(8,128)S(1)} %copy-done.1), custom_call_target="tpu_custom_call" | custom-call | tf_op jit(solution)/shard_map/pallas_call | solution.py:237
  93.2 0.6 broadcast_multiply_fusion
  (1 shorter events, 0.0 us)
Async XLA Ops:
  0.0 0.8 copy-start
  0.8 6.5 %copy-start.3 = (s32[32]{0:T(128)S(1)}, s32[32]{0:T(128)}, u32[]{:S(2)}) copy-start(s32[32]{0:T(128)} %param.7) | copy-start | bytes 388
  0.8 7.0 %copy-start.2 = (s32[32,512]{1,0:T(8,128)S(1)}, s32[32,512]{1,0:T(8,128)}, u32[]{:S(2)}) copy-start(s32[32,512]{1,0:T(8,128)} %param.6) | copy-start | bytes 196612
  4.1 55.9 %collective-permute-start = (f32[4,128,256]{2,1,0:T(8,128)S(1)}, f32[4,128,256]{2,1,0:T(8,128)S(1)}, u32[]{:S(2)}, u32[]{:S(2)}) collective-permute-start(f32[4,128,256]{2,1,0:T(8,128)S(1)} %get-tuple-element.9), channel_id=1, source_target_pairs={{0,1},{1,0},{2,3},{3,2},{4,5},{5,4},{6,7},{7,6},{8,9},{9,8},{10,11... | collective-permute-start | bytes 1572872 | tf_op jit(solution)/shard_map/ppermute | solution.py:292
  4.6 55.3 %collective-permute-start.1 = (f32[4,128,256]{2,1,0:T(8,128)S(1)}, f32[4,128,256]{2,1,0:T(8,128)S(1)}, u32[]{:S(2)}, u32[]{:S(2)}) collective-permute-start(f32[4,128,256]{2,1,0:T(8,128)S(1)} %get-tuple-element.10), channel_id=1, source_target_pairs={{0,2},{1,3},{2,0},{3,1},{4,6},{5,7},{6,4},{7,5},{8,10},{9,11},{10,... | collective-permute-start | bytes 1572872 | tf_op jit(solution)/shard_map/ppermute | solution.py:292
  7.2 52.8 %collective-permute-start.2 = (f32[4,128,256]{2,1,0:T(8,128)S(1)}, f32[4,128,256]{2,1,0:T(8,128)S(1)}, u32[]{:S(2)}, u32[]{:S(2)}) collective-permute-start(f32[4,128,256]{2,1,0:T(8,128)S(1)} %get-tuple-element.11), channel_id=1, source_target_pairs={{0,3},{1,2},{2,1},{3,0},{4,7},{5,6},{6,5},{7,4},{8,11},{9,10},{10,... | collective-permute-start | bytes 1572872 | tf_op jit(solution)/shard_map/ppermute | solution.py:292
  59.9 1.6 %copy-start.1 = (f32[16,256,128]{2,1,0:T(8,128)S(1)}, f32[16,256,128]{2,1,0:T(8,128)}, u32[]{:S(2)}) copy-start(f32[16,256,128]{2,1,0:T(8,128)} %shard_map.64.part_ref) | copy-start | bytes 6291460

commit v4 on v3

--- a/solution.py
+++ b/solution.py
@@ -8,8 +8,8 @@
 from jax.sharding import PartitionSpec as P
 
 LANES = 128
-UNROLL = 8
-PAD = 8
+UNROLL = 16
+PAD = 16
 CHUNK = 640
 
 
@@ -63,10 +63,10 @@
                 lax.fori_loop(tiles, steps_out // UNROLL, clear, 0)
 
                 def fetch(i, _):
-                    start = i * (2 * UNROLL)
+                    start = rec * (2 * steps_out) + i * (2 * UNROLL)
                     for u in range(UNROLL):
-                        even = ids_ref[rec, start + 2 * u]
-                        odd = ids_ref[rec, start + 2 * u + 1]
+                        even = ids_ref[start + 2 * u]
+                        odd = ids_ref[start + 2 * u + 1]
                         at = pl.ds(PAD + i * UNROLL + u, 1)
                         near[side, at, :] = rows[0, pl.ds(even, 1), :] + rows[1, pl.ds(odd, 1), :]
                         far[side, at, :] = rows[2, pl.ds(even, 1), :]
@@ -118,7 +118,8 @@
 
 def share_kernel(dp_count, left_ref, left_b, left_c, left_d, part_ref, out_ref, core_in, core_own, cross_out, cross_in,
                  planes, packed, every, sums, got, core_send, core_recv, cross_send, cross_recv,
-                 slice_send, slice_recv, wide_send, wide_recv, row_send, row_recv):
+                 slice_send, slice_recv, wide_send, wide_recv, row_send, row_recv,
+                 held, keep_sem, pass_send, pass_recv):
     me = lax.axis_index("tensor")
     block = lax.axis_index("dp")
     sib = me + 1 - 2 * (me % 2)
@@ -132,9 +133,17 @@
     barrier = pltpu.get_barrier_semaphore()
     for off in range(1, 4):
         pl.semaphore_signal(barrier, inc=1, device_id={"tensor": (me + off) % 4}, device_id_type=mesh_ids)
-    for off in range(1, dp_count):
-        pl.semaphore_signal(barrier, inc=1, device_id={"dp": (block + off) % dp_count}, device_id_type=mesh_ids)
-    pl.semaphore_wait(barrier, 3 + dp_count - 1)
+    inner = block + 1 - 2 * (block % 2)
+    hops = dp_count // 2
+    for peer in [inner] + [(block + 2 * off) % dp_count for off in range(1, hops)]:
+        pl.semaphore_signal(barrier, inc=1, device_id={"dp": peer}, device_id_type=mesh_ids)
+    keep = [
+        pltpu.make_async_copy(part_ref.at[pl.ds(owner * pairs, pairs)], held.at[k], keep_sem.at[k])
+        for k, owner in enumerate((across, me))
+    ]
+    for copy in keep:
+        copy.start()
+    pl.semaphore_wait(barrier, 3 + hops)
 
     def remote(src, dst, send, recv, where):
         return pltpu.make_async_remote_copy(
@@ -156,16 +165,18 @@
         remote(cross_out.at[i], cross_in.at[i], cross_send.at[i], cross_recv.at[i], {"tensor": across})
         for i in range(pairs)
     ]
+    keep[0].wait()
     for i in range(pairs):
         first[i].wait_recv()
-        cross_out[i] = (part_ref[across * pairs + i] + core_in[i]).astype(jnp.bfloat16)
+        cross_out[i] = (held[0, i] + core_in[i]).astype(jnp.bfloat16)
         over[i].start()
 
     lane = lax.broadcasted_iota(jnp.int32, (half // 2, LANES), 1) < half
     quarter = half // 2
+    keep[1].wait()
     for i in range(pairs):
         second[i].wait_recv()
-        mine = part_ref[me * pairs + i] + core_own[i]
+        mine = held[1, i] + core_own[i]
         over[i].wait_recv()
         right = mine + cross_in[i].astype(jnp.float32)
         raw = lax.dot_general(
@@ -195,12 +206,21 @@
         copy.wait_recv()
     wide = [
         remote(every.at[block], every.at[block], wide_send.at[off - 1], wide_recv.at[off - 1],
-               {"dp": (block + off) % dp_count})
-        for off in range(1, dp_count)
+               {"dp": (block + 2 * off) % dp_count})
+        for off in range(1, hops)
     ]
     for copy in wide:
         copy.start()
-    for copy in wide:
+    pass_on = []
+    for off in range(hops):
+        source = (block + 2 * (hops - off)) % dp_count
+        pass_on.append(
+            remote(every.at[source], every.at[source], pass_send.at[off], pass_recv.at[off], {"dp": inner})
+        )
+        if off > 0:
+            wide[off - 1].wait_recv()
+        pass_on[off].start()
+    for copy in pass_on:
         copy.wait_recv()
 
     recs = packed.shape[2]
@@ -224,7 +244,7 @@
         rows[off].wait_recv()
         result = result + got[off]
     out_ref[...] = result
-    for copy in first + second + over + slices + wide + rows:
+    for copy in first + second + over + slices + wide + pass_on + rows:
         copy.wait_send()
 
 
@@ -237,7 +257,7 @@
     return pl.pallas_call(
         functools.partial(share_kernel, dp_count),
         out_shape=jax.ShapeDtypeStruct((recs, dp_count * 4 * recs), jnp.float32),
-        in_specs=[vmem] * 5,
+        in_specs=[vmem] * 4 + [pl.BlockSpec(memory_space=pl.ANY)],
         out_specs=vmem,
         scratch_shapes=[
             pltpu.VMEM((pairs, steps_out, LANES), jnp.float32),
@@ -250,7 +270,9 @@
             pltpu.VMEM((4, recs, dp_count * 4 * recs), jnp.float32),
             pltpu.VMEM((3, recs, dp_count * 4 * recs), jnp.float32),
             dma((2 * pairs,)), dma((2 * pairs,)), dma((pairs,)), dma((pairs,)),
-            dma((3,)), dma((3,)), dma((dp_count - 1,)), dma((dp_count - 1,)), dma((3,)), dma((3,)),
+            dma((3,)), dma((3,)), dma((dp_count // 2 - 1,)), dma((dp_count // 2 - 1,)), dma((3,)), dma((3,)),
+            pltpu.VMEM((2, pairs, steps_out, LANES), jnp.float32),
+            dma((2,)), dma((dp_count // 2,)), dma((dp_count // 2,)),
         ],
         compiler_params=pltpu.CompilerParams(
             collective_id=0, has_side_effects=True, vmem_limit_bytes=40 * 1024 * 1024
@@ -275,7 +297,7 @@
     left_part = left_part_of(lengths, cotangent, proj_a)
 
     pos = jnp.arange(seqlen, dtype=jnp.int32)
-    ids = jnp.where(pos[None, :] < lengths[:, None], token_ids, vocab)
+    ids = jnp.where(pos[None, :] < lengths[:, None], token_ids, vocab).reshape(-1)
     live = (lengths + 1) // 2
     weights = jnp.transpose(proj_b, (1, 2, 0))
     if lax.axis_size("tensor") == 4:

time: 95.1 us -> 74 us (0.78)
  Pallas kernels: 83.1 us -> 62.2 us
    pallas_call x1, Pallas kernels: 51.5 us -> 32.1 us  [right_pairs(): pl.pallas_call(functools.partial(right_kernel, vocab, vblocks, group, ste...]
    pallas_call x1, Pallas kernels: 31.6 us -> 30.1 us  [share(): pl.pallas_call(functools.partial(share_kernel, dp_count), out_shape=jax.S...]
    unnamed x8 -> x9, local copies, waits for them, and re-layouts: 1.61 us -> 2.25 us
  transfers between devices with their start and end apart: 3 -> 3, of which waited for: 0 -> 0; matrix products, arithmetic and copies ran while one was open for 1% -> 2% of each run, Pallas kernels for 55% -> 44%
where the time goes in v4:
time: 74 us; the launch traced here: 72.8 us
  Pallas kernels  62.2 us (84%)
  starting transfers between devices  3.15 us (4%)
  matrix products  3.07 us (4%)
  local copies, waits for them, and re-layouts  2.46 us (3%)
  other arithmetic  1.94 us (3%)
    pallas_call x1, Pallas kernels, right_pairs(): pl.pallas_call(functools.partial(right_kernel, vocab, vblocks, group, ste...  32.1 us
    pallas_call x1, Pallas kernels, share(): pl.pallas_call(functools.partial(share_kernel, dp_count), out_shape=jax.S...  30.1 us
    ppermute x3, starting transfers between devices, local(): lax.ppermute(gift, 'tensor', list(enumerate(to)))  3.15 us
    dot_general x1, matrix products, left_part_of(): jnp.einsum('nct,ca->nat', masked, proj_a, preferred_element_type=jnp.floa...  3.07 us
    unnamed x9, local copies, waits for them, and re-layouts  2.25 us
  transfers between devices with their start and end apart: 3, of which 0 were waited for; matrix products, arithmetic and copies ran while one was open for 2% of the time, Pallas kernels for 44%

profile of v4, /device:TPU:0, one launch (start us, length us, event | category | flops | bytes accessed | tf_op | source)
XLA Modules:
  0.0 72.8 jit_solution(2069431198944104578)
XLA Ops:
  0.0 0.0 copy-start
  0.0 0.7 %broadcast_compare_fusion = pred[32,256]{1,0:T(8,128)(4,1)S(1)} fusion(s32[256]{0:T(256)S(1)} %iota_multiply_fusion, s32[32]{0:T(128)} %param.7), kind=kLoop, calls=%fused_computation.11 | loop fusion | flops 8192 | bytes 9344 | tf_op jit(solution)/shard_map/lt | solution.py:286
  0.7 0.0 copy-done
  0.8 0.0 copy-start.3
  0.8 0.0 copy-start.2
  0.8 3.1 %fusion = f32[32,256,64]{1,2,0:T(8,128)S(1)} fusion(bf16[32,256,256]{2,1,0:T(8,128)(2,1)} %param.9, pred[32,256]{1,0:T(8,128)(4,1)S(1)} %broadcast_compare_fusion, bf16[256,64]{0,1:T(8,128)(2,1)S(1)} %copy-done), kind=kOutput, calls=%fused_computation | convolution fusion | flops 270532608 | bytes 6332416 | tf_op jit(solution)/shard_map/nct,ca->nat/dot_general | solution.py:288
  3.9 0.2 dynamic-slice_bitcast_fusion
  4.1 0.5 collective-permute-start
  4.6 2.6 %collective-permute-start.1 = (f32[4,128,256]{2,1,0:T(8,128)S(1)}, f32[4,128,256]{2,1,0:T(8,128)S(1)}, u32[]{:S(2)}, u32[]{:S(2)}) collective-permute-start(f32[4,128,256]{2,1,0:T(8,128)S(1)} %get-tuple-element.10), channel_id=1, source_target_pairs={{0,2},{1,3},{2,0},{3,1},{4,6},{5,7},{6,4},{7,5},{8,10},{9,11},{10,... | collective-permute-start | bytes 1572872 | tf_op jit(solution)/shard_map/ppermute | solution.py:314
  7.2 0.1 collective-permute-start.2
  7.2 0.0 copy-done.3
  7.2 0.5 and_select_fusion.live_ref
  7.7 0.0 copy-done.2
  7.7 0.1 select_bitcast_fusion
  7.8 0.6 copy.7
  8.5 32.1 %shard_map.64.part_ref = f32[16,256,128]{2,1,0:T(8,128)} custom-call(s32[16384]{0:T(1024)} %bitcast.19, s32[32]{0:T(128)} %and_select_fusion.live_ref, bf16[256,32000]{1,0:T(8,128)(2,1)} %table_ref.1, bf16[5,64,256]{2,1,0:T(8,128)(2,1)} %bitcast.20), custom_call_target="tpu_custom_call" | custom-call | flops 6291456000 | bytes 209715200 | tf_op jit(solution)/shard_map/pallas_call | solution.py:92
  40.5 0.0 collective-permute-done.left_b
  40.5 0.0 collective-permute-done.1.left_c
  40.5 0.0 collective-permute-done.2.left_d
  40.6 0.0 copy-start.1
  40.6 1.6 %copy-done.1 = f32[16,256,128]{2,1,0:T(8,128)S(1)} copy-done((f32[16,256,128]{2,1,0:T(8,128)S(1)}, f32[16,256,128]{2,1,0:T(8,128)}, u32[]{:S(2)}) %copy-start.1) | copy-done | bytes 2097176
  42.1 30.1 %shard_map.65 = f32[8,256]{1,0:T(8,128)S(1)} custom-call(f32[4,128,256]{2,1,0:T(8,128)S(1)} %get-tuple-element.16.left_ref, f32[4,128,256]{2,1,0:T(8,128)S(1)} %collective-permute-done.left_b, f32[4,128,256]{2,1,0:T(8,128)S(1)} %collective-permute-done.1.left_c, f32[4,128,256]{2,1,0:T(8,128)S(1)} %collective-permute-done.2.left_d, f32[16,256,128]{2,1,0:T(8,128)S(1)} %copy-done.1), custom_call_target="tpu_custom_call" | custom-call | tf_op jit(solution)/shard_map/pallas_call | solution.py:257
  72.2 0.6 broadcast_multiply_fusion
  (1 shorter events, 0.0 us)
Async XLA Ops:
  0.0 0.8 %copy-start = (bf16[256,64]{0,1:T(8,128)(2,1)S(1)}, bf16[256,64]{0,1:T(8,128)(2,1)}, u32[]{:S(2)}) copy-start(bf16[256,64]{0,1:T(8,128)(2,1)} %param.10) | copy-start | bytes 98308
  0.8 6.5 %copy-start.3 = (s32[32]{0:T(128)S(1)}, s32[32]{0:T(128)}, u32[]{:S(2)}) copy-start(s32[32]{0:T(128)} %param.7) | copy-start | bytes 388
  0.8 7.0 %copy-start.2 = (s32[32,512]{1,0:T(8,128)S(1)}, s32[32,512]{1,0:T(8,128)}, u32[]{:S(2)}) copy-start(s32[32,512]{1,0:T(8,128)} %param.6) | copy-start | bytes 196612
  4.1 36.5 %collective-permute-start = (f32[4,128,256]{2,1,0:T(8,128)S(1)}, f32[4,128,256]{2,1,0:T(8,128)S(1)}, u32[]{:S(2)}, u32[]{:S(2)}) collective-permute-start(f32[4,128,256]{2,1,0:T(8,128)S(1)} %get-tuple-element.9), channel_id=1, source_target_pairs={{0,1},{1,0},{2,3},{3,2},{4,5},{5,4},{6,7},{7,6},{8,9},{9,8},{10,11... | collective-permute-start | bytes 1572872 | tf_op jit(solution)/shard_map/ppermute | solution.py:314
  4.6 36.0 %collective-permute-start.1 = (f32[4,128,256]{2,1,0:T(8,128)S(1)}, f32[4,128,256]{2,1,0:T(8,128)S(1)}, u32[]{:S(2)}, u32[]{:S(2)}) collective-permute-start(f32[4,128,256]{2,1,0:T(8,128)S(1)} %get-tuple-element.10), channel_id=1, source_target_pairs={{0,2},{1,3},{2,0},{3,1},{4,6},{5,7},{6,4},{7,5},{8,10},{9,11},{10,... | collective-permute-start | bytes 1572872 | tf_op jit(solution)/shard_map/ppermute | solution.py:314
  7.2 33.4 %collective-permute-start.2 = (f32[4,128,256]{2,1,0:T(8,128)S(1)}, f32[4,128,256]{2,1,0:T(8,128)S(1)}, u32[]{:S(2)}, u32[]{:S(2)}) collective-permute-start(f32[4,128,256]{2,1,0:T(8,128)S(1)} %get-tuple-element.11), channel_id=1, source_target_pairs={{0,3},{1,2},{2,1},{3,0},{4,7},{5,6},{6,5},{7,4},{8,11},{9,10},{10,... | collective-permute-start | bytes 1572872 | tf_op jit(solution)/shard_map/ppermute | solution.py:314
  40.6 1.6 %copy-start.1 = (f32[16,256,128]{2,1,0:T(8,128)S(1)}, f32[16,256,128]{2,1,0:T(8,128)}, u32[]{:S(2)}) copy-start(f32[16,256,128]{2,1,0:T(8,128)} %shard_map.64.part_ref) | copy-start | bytes 6291460

commit v5 on v4

--- a/solution.py
+++ b/solution.py
@@ -8,8 +8,8 @@
 from jax.sharding import PartitionSpec as P
 
 LANES = 128
-UNROLL = 16
-PAD = 16
+UNROLL = 32
+PAD = 32
 CHUNK = 640
 
 
@@ -88,7 +88,7 @@
     recipes = live.shape[0]
     vblk = 5 * CHUNK
     vblocks = vocab // vblk
-    group = 4
+    group = 8
     return pl.pallas_call(
         functools.partial(right_kernel, vocab, vblocks, group, steps_out),
         grid_spec=pltpu.PrefetchScalarGridSpec(

time: 74 us -> 72.8 us (0.984); the launches traced: 72.8 us -> 72.6 us
  no operation moved by 1% of the time
where the time goes in v5:
time: 72.8 us; the launch traced here: 72.6 us
  Pallas kernels  61.9 us (85%)
  starting transfers between devices  3.15 us (4%)
  matrix products  3.07 us (4%)
  local copies, waits for them, and re-layouts  2.46 us (3%)
  other arithmetic  1.94 us (3%)
    pallas_call x1, Pallas kernels, right_pairs(): pl.pallas_call(functools.partial(right_kernel, vocab, vblocks, group, ste...  31.7 us
    pallas_call x1, Pallas kernels, share(): pl.pallas_call(functools.partial(share_kernel, dp_count), out_shape=jax.S...  30.2 us
    ppermute x3, starting transfers between devices, local(): lax.ppermute(gift, 'tensor', list(enumerate(to)))  3.15 us
    dot_general x1, matrix products, left_part_of(): jnp.einsum('nct,ca->nat', masked, proj_a, preferred_element_type=jnp.floa...  3.07 us
    unnamed x9, local copies, waits for them, and re-layouts  2.25 us
  transfers between devices with their start and end apart: 3, of which 0 were waited for; matrix products, arithmetic and copies ran while one was open for 2% of the time, Pallas kernels for 44%

profile of v5, /device:TPU:0, one launch (start us, length us, event | category | flops | bytes accessed | tf_op | source)
XLA Modules:
  0.0 72.6 jit_solution(2532337857509400821)
XLA Ops:
  0.0 0.0 copy-start
  0.0 0.7 %broadcast_compare_fusion = pred[32,256]{1,0:T(8,128)(4,1)S(1)} fusion(s32[256]{0:T(256)S(1)} %iota_multiply_fusion, s32[32]{0:T(128)} %param.7), kind=kLoop, calls=%fused_computation.11 | loop fusion | flops 8192 | bytes 9344 | tf_op jit(solution)/shard_map/lt | solution.py:286
  0.7 0.0 copy-done
  0.8 0.0 copy-start.3
  0.8 0.0 copy-start.2
  0.8 3.1 %fusion = f32[32,256,64]{1,2,0:T(8,128)S(1)} fusion(bf16[32,256,256]{2,1,0:T(8,128)(2,1)} %param.9, pred[32,256]{1,0:T(8,128)(4,1)S(1)} %broadcast_compare_fusion, bf16[256,64]{0,1:T(8,128)(2,1)S(1)} %copy-done), kind=kOutput, calls=%fused_computation | convolution fusion | flops 270532608 | bytes 6332416 | tf_op jit(solution)/shard_map/nct,ca->nat/dot_general | solution.py:288
  3.9 0.2 dynamic-slice_bitcast_fusion
  4.1 0.5 collective-permute-start
  4.6 2.6 %collective-permute-start.1 = (f32[4,128,256]{2,1,0:T(8,128)S(1)}, f32[4,128,256]{2,1,0:T(8,128)S(1)}, u32[]{:S(2)}, u32[]{:S(2)}) collective-permute-start(f32[4,128,256]{2,1,0:T(8,128)S(1)} %get-tuple-element.10), channel_id=1, source_target_pairs={{0,2},{1,3},{2,0},{3,1},{4,6},{5,7},{6,4},{7,5},{8,10},{9,11},{10,... | collective-permute-start | bytes 1572872 | tf_op jit(solution)/shard_map/ppermute | solution.py:314
  7.2 0.1 collective-permute-start.2
  7.2 0.0 copy-done.3
  7.2 0.5 and_select_fusion.live_ref
  7.7 0.0 copy-done.2
  7.7 0.1 select_bitcast_fusion
  7.8 0.6 copy.7
  8.5 31.7 %shard_map.64.part_ref = f32[16,256,128]{2,1,0:T(8,128)} custom-call(s32[16384]{0:T(1024)} %bitcast.19, s32[32]{0:T(128)} %and_select_fusion.live_ref, bf16[256,32000]{1,0:T(8,128)(2,1)} %table_ref.1, bf16[5,64,256]{2,1,0:T(8,128)(2,1)} %bitcast.20), custom_call_target="tpu_custom_call" | custom-call | flops 6291456000 | bytes 209715200 | tf_op jit(solution)/shard_map/pallas_call | solution.py:92
  40.2 0.0 collective-permute-done.left_b
  40.2 0.0 collective-permute-done.1.left_c
  40.2 0.0 collective-permute-done.2.left_d
  40.2 0.0 copy-start.1
  40.2 1.6 %copy-done.1 = f32[16,256,128]{2,1,0:T(8,128)S(1)} copy-done((f32[16,256,128]{2,1,0:T(8,128)S(1)}, f32[16,256,128]{2,1,0:T(8,128)}, u32[]{:S(2)}) %copy-start.1) | copy-done | bytes 2097176
  41.8 30.2 %shard_map.65 = f32[8,256]{1,0:T(8,128)S(1)} custom-call(f32[4,128,256]{2,1,0:T(8,128)S(1)} %get-tuple-element.16.left_ref, f32[4,128,256]{2,1,0:T(8,128)S(1)} %collective-permute-done.left_b, f32[4,128,256]{2,1,0:T(8,128)S(1)} %collective-permute-done.1.left_c, f32[4,128,256]{2,1,0:T(8,128)S(1)} %collective-permute-done.2.left_d, f32[16,256,128]{2,1,0:T(8,128)S(1)} %copy-done.1), custom_call_target="tpu_custom_call" | custom-call | tf_op jit(solution)/shard_map/pallas_call | solution.py:257
  72.0 0.6 broadcast_multiply_fusion
  (1 shorter events, 0.0 us)
Async XLA Ops:
  0.0 0.8 %copy-start = (bf16[256,64]{0,1:T(8,128)(2,1)S(1)}, bf16[256,64]{0,1:T(8,128)(2,1)}, u32[]{:S(2)}) copy-start(bf16[256,64]{0,1:T(8,128)(2,1)} %param.10) | copy-start | bytes 98308
  0.8 6.5 %copy-start.3 = (s32[32]{0:T(128)S(1)}, s32[32]{0:T(128)}, u32[]{:S(2)}) copy-start(s32[32]{0:T(128)} %param.7) | copy-start | bytes 388
  0.8 7.0 %copy-start.2 = (s32[32,512]{1,0:T(8,128)S(1)}, s32[32,512]{1,0:T(8,128)}, u32[]{:S(2)}) copy-start(s32[32,512]{1,0:T(8,128)} %param.6) | copy-start | bytes 196612
  4.1 36.1 %collective-permute-start = (f32[4,128,256]{2,1,0:T(8,128)S(1)}, f32[4,128,256]{2,1,0:T(8,128)S(1)}, u32[]{:S(2)}, u32[]{:S(2)}) collective-permute-start(f32[4,128,256]{2,1,0:T(8,128)S(1)} %get-tuple-element.9), channel_id=1, source_target_pairs={{0,1},{1,0},{2,3},{3,2},{4,5},{5,4},{6,7},{7,6},{8,9},{9,8},{10,11... | collective-permute-start | bytes 1572872 | tf_op jit(solution)/shard_map/ppermute | solution.py:314
  4.6 35.6 %collective-permute-start.1 = (f32[4,128,256]{2,1,0:T(8,128)S(1)}, f32[4,128,256]{2,1,0:T(8,128)S(1)}, u32[]{:S(2)}, u32[]{:S(2)}) collective-permute-start(f32[4,128,256]{2,1,0:T(8,128)S(1)} %get-tuple-element.10), channel_id=1, source_target_pairs={{0,2},{1,3},{2,0},{3,1},{4,6},{5,7},{6,4},{7,5},{8,10},{9,11},{10,... | collective-permute-start | bytes 1572872 | tf_op jit(solution)/shard_map/ppermute | solution.py:314
  7.2 33.0 %collective-permute-start.2 = (f32[4,128,256]{2,1,0:T(8,128)S(1)}, f32[4,128,256]{2,1,0:T(8,128)S(1)}, u32[]{:S(2)}, u32[]{:S(2)}) collective-permute-start(f32[4,128,256]{2,1,0:T(8,128)S(1)} %get-tuple-element.11), channel_id=1, source_target_pairs={{0,3},{1,2},{2,1},{3,0},{4,7},{5,6},{6,5},{7,4},{8,11},{9,10},{10,... | collective-permute-start | bytes 1572872 | tf_op jit(solution)/shard_map/ppermute | solution.py:314
  40.2 1.6 %copy-start.1 = (f32[16,256,128]{2,1,0:T(8,128)S(1)}, f32[16,256,128]{2,1,0:T(8,128)}, u32[]{:S(2)}) copy-start(f32[16,256,128]{2,1,0:T(8,128)} %shard_map.64.part_ref) | copy-start | bytes 6291460
